TPU v7x, 32 devices: a whole 2x2x4 slice. The times are simulated.
32 devices in a mesh: seq: 16 (over z, x, core), exp: 2 (over y).
Axes of the slice: x: 2, y: 2, z: 4, core: 2. Of those that a mesh axis runs over, the one named last changes fastest.
Arguments:
- tokens: bfloat16 [30720, 1024], P('seq'), may hold values from -24 to 24
- slot_embed: bfloat16 [1024, 512], P(None, 'exp'), may hold values from -3 to 3
- w_in: bfloat16 [32, 1024, 4096], P('exp', None, 'seq'), may hold values from -0.375 to 0.375
- w_out: bfloat16 [32, 4096, 1024], P('exp', 'seq'), may hold values from -0.125 to 0.125
Outputs:
- mixed_out: bfloat16 [30720, 1024], P('seq', 'exp')
All inputs are finite; a program needn't handle non-finite values.
Results may differ from a plain program's by a relative error of at most 0.012.
Values may be sent and summed in bfloat16 or wider, within the bound.
A program may use at most 64 MiB of HBM per device.

v0:
```python
import jax
import jax.numpy as jnp
from jax import lax
from jax.sharding import PartitionSpec as P


def joined(part, axis, combine):
    gathered = jax.tree.map(lambda a: lax.all_gather(a, axis), part)

    def take(source):
        return jax.tree.map(lambda a: lax.dynamic_index_in_dim(a, source, 0, False), gathered)

    return lax.fori_loop(
        1, lax.axis_size(axis), lambda source, state: combine(state, take(source)), take(0)
    )


def gelu_tanh(values):
    return (
        0.5
        * values
        * (1.0 + jnp.tanh(0.7978845608028654 * (values + 0.044715 * values * values * values)))
    )


def pair_max(earlier, later):
    peak = jnp.maximum(earlier[0], later[0])
    return (peak, earlier[1] * jnp.exp(earlier[0] - peak) + later[1] * jnp.exp(later[0] - peak))


def on_device(tokens, slot_embed, w_in, w_out):
    experts_here = w_in.shape[0]
    slot_count = slot_embed.shape[1]
    slot_exp = slot_count // experts_here
    features = tokens.shape[1]
    logits = jnp.dot(tokens, slot_embed, preferred_element_type=jnp.float32)
    col_peak = jnp.max(logits, axis=0)
    local_weights = jnp.exp(logits - col_peak[None, :])
    peak_all, total_all = joined((col_peak, jnp.sum(local_weights, axis=0)), "seq", pair_max)
    weights = local_weights * jnp.exp(col_peak - peak_all)[None, :]
    dispatch = (weights / total_all[None, :]).astype(jnp.bfloat16)
    partial_in = lax.dot_general(
        dispatch, tokens, (((0,), (0,)), ((), ())), preferred_element_type=jnp.float32
    )
    slot_in = lax.psum(partial_in, "seq").astype(jnp.bfloat16)
    grouped = slot_in.reshape(experts_here, slot_exp, features)
    hidden = gelu_tanh(
        jnp.einsum("esd,edh->esh", grouped, w_in, preferred_element_type=jnp.float32)
    ).astype(jnp.bfloat16)
    partial_out = jnp.einsum(
        "esh,ehd->esd", hidden, w_out, preferred_element_type=jnp.float32
    ).reshape(slot_count, features)
    slot_out = lax.psum(partial_out, "seq").astype(jnp.bfloat16)
    row_peak = lax.pmax(jnp.max(logits, axis=1), "exp")
    row_weights = jnp.exp(logits - row_peak[:, None])
    row_sum = lax.psum(jnp.sum(row_weights, axis=1), "exp")
    combine = (row_weights / row_sum[:, None]).astype(jnp.bfloat16)
    term = jnp.dot(combine, slot_out, preferred_element_type=jnp.float32)
    mixed_out = lax.psum_scatter(term.astype(jnp.bfloat16), "exp", scatter_dimension=1, tiled=True)
    return mixed_out


def solution(mesh):
    placed = (P("seq", None), P(None, "exp"), P("exp", None, "seq"), P("exp", "seq", None))
    return jax.shard_map(
        on_device, mesh=mesh, in_specs=placed, out_specs=P("seq", "exp"), check_vma=False
    )
```

profile of v0, /device:TPU:0, one launch (start us, length us, event | category | flops | bytes accessed | tf_op | source)
XLA Modules:
  0.0 275.3 jit_solution(14795030857905680253)
XLA Ops:
  6.5 0.0 copy-start
  6.5 0.0 reduce-scatter.2.cloned.1.call-start
  6.5 1.0 copy-done
  7.6 3.4 %fusion.24 = (f32[256]{0:T(256)S(1)}, f32[1920]{0:T(1024)S(1)}, f32[1920,256]{1,0:T(8,128)S(1)}) fusion(bf16[1920,1024]{1,0:T(8,128)(2,1)} %param.6, bf16[1024,256]{1,0:T(8,128)(2,1)S(1)} %copy-done), kind=kOutput, calls=%fused_computation.35 | convolution fusion | flops 1007613824 | bytes 6431232 | tf_op jit(solution)/shard_map/dot_general | solution.py:36
  11.0 0.0 copy-start.1
  11.0 6.0 %pmax.7 = f32[1920]{0:T(1024)S(1)} all-reduce(f32[1920]{0:T(1024)S(1)} %get-tuple-element.143), channel_id=1, replica_groups=mesh['seq'=16,'exp'=2] {'exp'}, use_global_device_ids=true, to_apply=%region_1.0 | all-reduce | flops 1920 | bytes 15360 | tf_op jit(solution)/shard_map/pmax | solution.py:54
  16.9 0.8 fusion.1
  17.7 22.2 %all-gather.3 = f32[16,1,256]{2,1,0:T(1,128)S(1)} all-gather(f32[1,1,256]{2,1,0:T(1,128)S(1)} %bitcast.34), channel_id=3, replica_groups=mesh['seq'=16,'exp'=2] {'seq'}, dimensions={0}, use_global_device_ids=true | all-gather | bytes 17408 | tf_op jit(solution)/shard_map/all_gather | solution.py:8
  39.9 17.4 %all-gather.2 = f32[16,1,256]{2,1,0:T(1,128)S(1)} all-gather(f32[1,1,256]{2,1,0:T(1,128)S(1)} %bitcast.33), channel_id=2, replica_groups=mesh['seq'=16,'exp'=2] {'seq'}, dimensions={0}, use_global_device_ids=true | all-gather | bytes 17408 | tf_op jit(solution)/shard_map/all_gather | solution.py:8
  57.3 5.6 %psum.21 = f32[1920]{0:T(1024)} all-reduce(f32[1920]{0:T(1024)S(1)} %get-tuple-element.141), channel_id=1, replica_groups=mesh['seq'=16,'exp'=2] {'exp'}, use_global_device_ids=true, to_apply=%region_3.4 | all-reduce | flops 1920 | bytes 15360 | tf_op jit(solution)/shard_map/psum | solution.py:56
  62.9 0.8 while.17
  63.7 0.0 copy-done.1
  63.8 3.4 %fusion.2 = f32[256,1024]{1,0:T(8,128)S(1)} fusion(bf16[1920,1024]{1,0:T(8,128)(2,1)} %param.6, f32[1920,256]{1,0:T(8,128)S(1)} %get-tuple-element.158, f32[256]{0:T(256)S(1)} %get-tuple-element.139, f32[256]{0:T(256)S(1)} %subtract_exponential_fusion.2, f32[256]{0:T(256)S(1)} %get-tuple-element.142), kind=kOutput, calls=%fused_computation.10 | convolution fusion | flops 1008599040 | bytes 6949888 | tf_op jit(solution)/shard_map/dot_general | solution.py:42
  67.2 69.7 %all-reduce.2 = bf16[256,1024]{1,0:T(8,128)(2,1)S(1)} all-reduce(f32[256,1024]{1,0:T(8,128)S(1)} %fusion.2), channel_id=1, replica_groups=mesh['seq'=16,'exp'=2] {'seq'}, use_global_device_ids=true, to_apply=%region_8.9 | all-reduce | flops 262144 | bytes 1572864 | tf_op jit(solution)/shard_map/psum | solution.py:45
  136.8 0.0 copy-start.2
  136.8 8.1 %fusion.14 = f32[16,16,1024]{2,1,0:T(8,128)S(1)} fusion(bf16[16,256,1024]{2,1,0:T(8,128)(2,1)} %param.9, bf16[16,16,1024]{2,1,0:T(8,128)(2,1)S(1)} %bitcast.26, bf16[16,1024,256]{2,1,0:T(8,128)(2,1)} %param.8), kind=kOutput, calls=%fused_computation.23 | convolution fusion | flops 269025280 | bytes 18350080 | tf_op jit(solution)/shard_map/esh,ehd->esd/dot_general | solution.py:50
  144.9 69.3 %all-reduce.3 = bf16[256,1024]{1,0:T(8,128)(2,1)S(1)} all-reduce(f32[256,1024]{1,0:T(8,128)S(1)} %bitcast.25), channel_id=1, replica_groups=mesh['seq'=16,'exp'=2] {'seq'}, use_global_device_ids=true, to_apply=%region_9.10 | all-reduce | flops 262144 | bytes 1572864 | tf_op jit(solution)/shard_map/psum | solution.py:53
  214.2 0.0 copy-done.2
  214.2 4.7 %convolution_convert_fusion = bf16[1920,1024]{1,0:T(8,128)(2,1)} fusion(f32[1920,256]{1,0:T(8,128)} %copy-done.1, f32[1920]{0:T(1024)S(1)} %copy-done.2, f32[1920]{0:T(1024)S(1)} %pmax.7, bf16[256,1024]{1,0:T(8,128)(2,1)S(1)} %all-reduce.3), kind=kOutput, calls=%fused_computation.3 | convolution fusion | flops 1010073600 | bytes 6437888 | tf_op jit(solution)/shard_map/dot_general | solution.py:58
  218.9 0.0 reduce-scatter.2.cloned.1.call-update
  219.0 49.5 %reduce-scatter.2.cloned.1.call-done = bf16[1920,512]{1,0:T(8,128)(2,1)} async-done(((bf16[1920,1024]{1,0:T(8,128)(2,1)}), bf16[1920,512]{1,0:T(8,128)(2,1)}) %reduce-scatter.2.cloned.1.call-update) | async-done | bytes 1966096 | tf_op jit(solution)/shard_map/reduce_scatter | solution.py:59
  (35 shorter events, 0.5 us)
Async XLA Ops:
  6.5 1.0 copy-start
  6.5 261.9 %reduce-scatter.2.cloned.1.call-start = ((), (), s32[]{:S(2)}) async-start(), calls=%async_computation.1 | async-start | bytes 5898240 | tf_op jit(solution)/shard_map/reduce_scatter | solution.py:59
  11.0 52.8 %copy-start.1 = (f32[1920,256]{1,0:T(8,128)}, f32[1920,256]{1,0:T(8,128)S(1)}, u32[]{:S(2)}) copy-start(f32[1920,256]{1,0:T(8,128)S(1)} %get-tuple-element.158) | copy-start | bytes 5898244
  136.8 77.4 %copy-start.2 = (f32[1920]{0:T(1024)S(1)}, f32[1920]{0:T(1024)}, u32[]{:S(2)}) copy-start(f32[1920]{0:T(1024)} %psum.21) | copy-start | bytes 23044
Sparse Core Ops, SparseCore 0:
  219.1 49.3 reduce-scatter.1
where the time goes:
time: 276 us; the launch traced here: 275 us
  blocking collectives  190 us (69%)
  waiting for transfers between devices  49.5 us (18%)
  matrix products  19.6 us (7%)
  between operations  13.5 us (5%)
    psum x1, blocking collectives, on_device(): slot_in = lax.psum(partial_in, 'seq').astype(jnp.bfloat16)  69.7 us
    psum x1, blocking collectives, on_device(): slot_out = lax.psum(partial_out, 'seq').astype(jnp.bfloat16)  69.3 us
    reduce_scatter x1, waiting for transfers between devices, on_device(): lax.psum_scatter(term.astype(jnp.bfloat16), 'exp', scatter_dimension=1, t...  49.5 us
    all_gather x2, blocking collectives, joined(): gathered = jax.tree.map(lambda a: lax.all_gather(a, axis), part)  39.6 us
    dot_general x1, matrix products, on_device(): jnp.einsum('esh,ehd->esd', hidden, w_out, preferred_element_type=jnp.floa...  8.06 us
    pmax x1, blocking collectives, on_device(): row_peak = lax.pmax(jnp.max(logits, axis=1), 'exp')  5.97 us
    psum x1, blocking collectives, on_device(): row_sum = lax.psum(jnp.sum(row_weights, axis=1), 'exp')  5.56 us
  transfers between devices with their start and end apart: 1, of which 1 were waited for; matrix products, arithmetic and copies ran while one was open for 0% of the time, Pallas kernels for 0%

commit v1 on v0

--- a/solution.py
+++ b/solution.py
@@ -42,7 +42,7 @@
     partial_in = lax.dot_general(
         dispatch, tokens, (((0,), (0,)), ((), ())), preferred_element_type=jnp.float32
     )
-    slot_in = lax.psum(partial_in, "seq").astype(jnp.bfloat16)
+    slot_in = jnp.sum(lax.all_gather(partial_in, "seq"), axis=0).astype(jnp.bfloat16)
     grouped = slot_in.reshape(experts_here, slot_exp, features)
     hidden = gelu_tanh(
         jnp.einsum("esd,edh->esh", grouped, w_in, preferred_element_type=jnp.float32)

time: 276 us -> 335 us (1.21)
  waiting for transfers between devices: 49.5 us -> 169 us
  blocking collectives: 190 us -> 121 us
  other arithmetic: 1.1 us -> 8.82 us
    all_gather x0 -> x1, waiting for transfers between devices: none -> 120 us  [on_device(): lax.all_gather(partial_in, 'seq')]
    psum x1 -> x0, blocking collectives: 69.7 us -> none  [on_device(): slot_in = lax.psum(partial_in, 'seq').astype(jnp.bfloat16)]
    reduce_sum x0 -> x1, other arithmetic: none -> 7.72 us  [on_device(): jnp.sum(lax.all_gather(partial_in, 'seq'), axis=0).astype(jnp.bfloat16)]
  transfers between devices with their start and end apart: 1 -> 2, of which waited for: 1 -> 2; matrix products, arithmetic and copies ran while one was open for 0% -> 0% of each run, Pallas kernels for 0% -> 0%
where the time goes in v1:
time: 335 us
  waiting for transfers between devices  169 us (50%)
  blocking collectives  121 us (36%)
  matrix products  20.6 us (6%)
  between operations  13.4 us (4%)
  other arithmetic  8.82 us (3%)
    all_gather x1, waiting for transfers between devices, on_device(): lax.all_gather(partial_in, 'seq')  120 us
    psum x1, blocking collectives, on_device(): slot_out = lax.psum(partial_out, 'seq').astype(jnp.bfloat16)  70.6 us
    reduce_scatter x1, waiting for transfers between devices, on_device(): lax.psum_scatter(term.astype(jnp.bfloat16), 'exp', scatter_dimension=1, t...  49.5 us
    all_gather x2, blocking collectives, joined(): gathered = jax.tree.map(lambda a: lax.all_gather(a, axis), part)  39.6 us
    dot_general x1, matrix products, on_device(): jnp.einsum('esh,ehd->esd', hidden, w_out, preferred_element_type=jnp.floa...  8.06 us
    reduce_sum x1, other arithmetic, on_device(): jnp.sum(lax.all_gather(partial_in, 'seq'), axis=0).astype(jnp.bfloat16)  7.72 us
  transfers between devices with their start and end apart: 2, of which 2 were waited for; matrix products, arithmetic and copies ran while one was open for 0% of the time, Pallas kernels for 0%

profile of v1, /device:TPU:0, one launch (start us, length us, event | category | flops | bytes accessed | tf_op | source)
XLA Modules:
  0.0 335.1 jit_solution(5972862360933960799)
XLA Ops:
  6.5 0.0 copy-start
  6.5 0.0 all-gather.7.cloned.1.call-start
  6.5 1.0 copy-done
  7.6 3.4 %fusion.24 = (f32[256]{0:T(256)S(1)}, f32[1920]{0:T(1024)S(1)}, f32[1920,256]{1,0:T(8,128)S(1)}) fusion(bf16[1920,1024]{1,0:T(8,128)(2,1)} %param.6, bf16[1024,256]{1,0:T(8,128)(2,1)S(1)} %copy-done), kind=kOutput, calls=%fused_computation.35 | convolution fusion | flops 1007613824 | bytes 6431232 | tf_op jit(solution)/shard_map/dot_general | solution.py:36
  11.0 0.0 copy-start.1
  11.0 6.0 %pmax.7 = f32[1920]{0:T(1024)S(1)} all-reduce(f32[1920]{0:T(1024)S(1)} %get-tuple-element.143), channel_id=1, replica_groups=mesh['seq'=16,'exp'=2] {'exp'}, use_global_device_ids=true, to_apply=%region_1.0 | all-reduce | flops 1920 | bytes 15360 | tf_op jit(solution)/shard_map/pmax | solution.py:54
  16.9 0.8 fusion.1
  17.7 22.2 %all-gather.4 = f32[16,1,256]{2,1,0:T(1,128)S(1)} all-gather(f32[1,1,256]{2,1,0:T(1,128)S(1)} %bitcast.36), channel_id=3, replica_groups=mesh['seq'=16,'exp'=2] {'seq'}, dimensions={0}, use_global_device_ids=true | all-gather | bytes 17408 | tf_op jit(solution)/shard_map/all_gather | solution.py:8
  39.9 17.4 %all-gather.3 = f32[16,1,256]{2,1,0:T(1,128)S(1)} all-gather(f32[1,1,256]{2,1,0:T(1,128)S(1)} %bitcast.35), channel_id=2, replica_groups=mesh['seq'=16,'exp'=2] {'seq'}, dimensions={0}, use_global_device_ids=true | all-gather | bytes 17408 | tf_op jit(solution)/shard_map/all_gather | solution.py:8
  57.3 0.8 while.17
  58.2 4.4 %fusion.2 = f32[256,1024]{1,0:T(8,128)} fusion(bf16[1920,1024]{1,0:T(8,128)(2,1)} %param.6, f32[1920,256]{1,0:T(8,128)S(1)} %get-tuple-element.158, f32[256]{0:T(256)S(1)} %get-tuple-element.139, f32[256]{0:T(256)S(1)} %subtract_exponential_fusion.2, f32[256]{0:T(256)S(1)} %get-tuple-element.142), kind=kOutput, calls=%fused_computation.10 | convolution fusion | flops 1008599040 | bytes 6949888 | tf_op jit(solution)/shard_map/dot_general | solution.py:42
  62.6 0.0 copy-done.1
  62.6 0.0 all-gather.7.cloned.1.call-update
  62.6 0.0 reduce-scatter.2.cloned.1.call-start
  62.7 5.0 %psum.14 = f32[1920]{0:T(1024)S(1)} all-reduce(f32[1920]{0:T(1024)S(1)} %get-tuple-element.141), channel_id=1, replica_groups=mesh['seq'=16,'exp'=2] {'exp'}, use_global_device_ids=true, to_apply=%region_3.4 | all-reduce | flops 1920 | bytes 15360 | tf_op jit(solution)/shard_map/psum | solution.py:56
  67.7 119.9 %all-gather.7.cloned.1.call-done = f32[4096,1024]{1,0:T(8,128)} async-done(((f32[256,1024]{1,0:T(8,128)}), f32[4096,1024]{1,0:T(8,128)}) %all-gather.7.cloned.1.call-update) | async-done | bytes 16777232 | tf_op jit(solution)/shard_map/all_gather | solution.py:45
  187.6 7.7 %reduce_sum.29 = bf16[256,1024]{1,0:T(8,128)(2,1)S(1)} reduce(f32[16,256,1024]{2,1,0:T(8,128)} %bitcast.26, f32[]{:T(128)} %constant.53.clone.1), dimensions={0}, to_apply=%region_8.9 | reduce | flops 3932160 | bytes 17301508 | tf_op jit(solution)/shard_map/reduce_sum | solution.py:45
  195.4 8.1 %fusion.14 = f32[16,16,1024]{2,1,0:T(8,128)S(1)} fusion(bf16[16,256,1024]{2,1,0:T(8,128)(2,1)} %param.9, bf16[16,16,1024]{2,1,0:T(8,128)(2,1)S(1)} %bitcast.28, bf16[16,1024,256]{2,1,0:T(8,128)(2,1)} %param.8), kind=kOutput, calls=%fused_computation.23 | convolution fusion | flops 269025280 | bytes 18350080 | tf_op jit(solution)/shard_map/esh,ehd->esd/dot_general | solution.py:50
  203.4 70.6 %all-reduce.1 = bf16[256,1024]{1,0:T(8,128)(2,1)S(1)} all-reduce(f32[256,1024]{1,0:T(8,128)S(1)} %bitcast.27), channel_id=1, replica_groups=mesh['seq'=16,'exp'=2] {'seq'}, use_global_device_ids=true, to_apply=%region_9.10 | all-reduce | flops 262144 | bytes 1572864 | tf_op jit(solution)/shard_map/psum | solution.py:53
  274.0 4.7 %convolution_convert_fusion = bf16[1920,1024]{1,0:T(8,128)(2,1)} fusion(f32[1920,256]{1,0:T(8,128)} %copy-done.1, f32[1920]{0:T(1024)S(1)} %psum.14, f32[1920]{0:T(1024)S(1)} %pmax.7, bf16[256,1024]{1,0:T(8,128)(2,1)S(1)} %all-reduce.1), kind=kOutput, calls=%fused_computation.3 | convolution fusion | flops 1010073600 | bytes 6437888 | tf_op jit(solution)/shard_map/dot_general | solution.py:58
  278.7 0.0 reduce-scatter.2.cloned.1.call-update
  278.8 49.5 %reduce-scatter.2.cloned.1.call-done = bf16[1920,512]{1,0:T(8,128)(2,1)} async-done(((bf16[1920,1024]{1,0:T(8,128)(2,1)}), bf16[1920,512]{1,0:T(8,128)(2,1)}) %reduce-scatter.2.cloned.1.call-update) | async-done | bytes 1966096 | tf_op jit(solution)/shard_map/reduce_scatter | solution.py:59
  (35 shorter events, 0.5 us)
Async XLA Ops:
  6.5 1.0 copy-start
  6.5 181.1 %all-gather.7.cloned.1.call-start = ((), (), s32[]{:S(2)}) async-start(), calls=%async_computation.2 | async-start | bytes 17825792 | tf_op jit(solution)/shard_map/all_gather | solution.py:45
  11.0 51.6 %copy-start.1 = (f32[1920,256]{1,0:T(8,128)}, f32[1920,256]{1,0:T(8,128)S(1)}, u32[]{:S(2)}) copy-start(f32[1920,256]{1,0:T(8,128)S(1)} %get-tuple-element.158) | copy-start | bytes 5898244
  62.6 265.6 %reduce-scatter.2.cloned.1.call-start = ((), (), s32[]{:S(2)}) async-start(), calls=%async_computation.1 | async-start | bytes 5898240 | tf_op jit(solution)/shard_map/reduce_scatter | solution.py:59
Sparse Core Ops, SparseCore 0:
  62.7 124.8 all-gather.6
  278.9 49.3 reduce-scatter.1
